TPU v7x, 256 devices: a whole 4x4x8 slice. The times are simulated.
256 devices in a mesh: wide: 32 (over x, y, core), narrow: 8 (over z).
Axes of the slice: x: 4, y: 4, z: 8, core: 2. Of those that a mesh axis runs over, the one named last changes fastest.
Arguments:
- sources: float32 [32, 8, 16, 2, 512], P('wide', 'narrow'), may hold values from -6 to 6
- schur_blocks: bfloat16 [32, 8, 2048, 2048], P('wide', 'narrow'), as said below
- scaling: float32 [32, 8, 2, 512], P('wide', 'narrow'), may hold values from 0.08 to 0.4
- coarse_basis: float32 [32, 8, 2, 2, 8, 512], P('wide', 'narrow'), may hold values from -0.09375 to 0.09375
- coarse_inverse: float32 [32, 80, 80], P('wide'), as said below
- face_sizes: int32 [32, 8, 2], P('wide', 'narrow'), may hold values from 0 to 512, as said below
- face_match: int32 [32, 8, 2, 512], P('wide', 'narrow'), may hold values from 0 to 511, as said below
- face_slots: int32 [32, 8, 4], P('wide', 'narrow'), may hold values from 0 to 3, each once within a row
- corner_slots: int32 [33, 9], replicated, may hold values from 0 to 319, as said below
Outputs:
- solution: float32 [32, 8, 16, 2, 512], P('wide', 'narrow')
- residual: float32 [32, 8, 16, 2, 512], P('wide', 'narrow')
Inputs may be any that keep to these rules, and one draw needn't show every extreme that they name: `face_sizes`: the east faces of the last wide index and the north faces of the last narrow index have 0 unknowns; every other face has 128 to 512, and some face has exactly 512. `face_match`: each block is a permutation of 0 to 511 that maps the positions below the size of the matching owned face onto themselves. `corner_slots`: distinct slots for distinct vertices; slot 319 is used. `schur_blocks`: each block is symmetric and positive definite. `coarse_inverse`: each block is symmetric and positive definite.
All inputs are finite; a program needn't handle non-finite values.
Results may differ from a plain program's by a relative error of at most 0.0052.
Values may be sent and summed in bfloat16 or wider, within the bound.
A program may use at most 64 MiB of HBM per device.

v0:
```python
import jax
import jax.numpy as jnp
from jax import lax
from jax.sharding import PartitionSpec as P

ITERS = 2
highest = lax.Precision.HIGHEST


def shifted(block, axis, distance):
    devices = range(lax.axis_size(axis))
    route = [(i - distance, i) for i in devices if i - distance in devices]
    return lax.ppermute(block, axis, route)


def body(
    sources,
    schur_blocks,
    scaling,
    coarse_basis,
    coarse_inverse,
    face_sizes,
    face_match,
    face_slots,
    corner_slots,
):
    wide_count = lax.axis_size("wide")
    wide_at = lax.axis_index("wide")
    narrow_at = lax.axis_index("narrow")
    nrhs_count = sources.shape[2]
    face_width = sources.shape[4]
    basis_count = coarse_basis.shape[4]
    block_order = coarse_inverse.shape[1]
    capacity = block_order // basis_count
    slot_count = capacity * wide_count
    places = lax.broadcasted_iota(jnp.int32, (2, face_width), 1)
    live_mask = (places < face_sizes[0, 0][:, None]).astype(jnp.float32)
    weights = scaling[0, 0] * live_mask
    vectors = coarse_basis[0, 0] * live_mask[:, None, None, :]
    forward = face_match[0, 0]
    source_rows = lax.broadcasted_iota(jnp.int32, (2, face_width, face_width), 1)
    match_table = (forward[:, None, :] == source_rows).astype(jnp.float32)
    match_narrow = match_table.astype(jnp.bfloat16)
    slot_table = (face_slots[0, 0][:, None] == jnp.arange(4, dtype=jnp.int32)[None, :]).astype(
        jnp.float32
    )
    matrix = schur_blocks[0, 0]
    square = lax.dynamic_slice(corner_slots, (wide_at, narrow_at), (2, 2))
    corner_ids = jnp.stack([square[1, 0], square[1, 1], square[0, 1], square[1, 1]])
    incidence = (corner_ids[:, None] == jnp.arange(slot_count, dtype=jnp.int32)[None, :]).astype(
        jnp.float32
    )
    inverse_block = coarse_inverse[0]
    initial = sources[0, 0] * live_mask[None]

    def finish(residual, solved_slots):
        local_values = jnp.dot(
            incidence, solved_slots, precision=highest, preferred_element_type=jnp.float32
        )
        local_values = local_values.reshape(2, 2, basis_count, nrhs_count)
        return weights[None] * residual + jnp.einsum(
            "femk,femr->rfk", vectors, local_values, precision=highest
        )

    def precondition(residual):
        partial_value = jnp.einsum("femk,rfk->femr", vectors, residual, precision=highest).reshape(
            4, basis_count * nrhs_count
        )
        dense_part = jnp.dot(
            incidence.T, partial_value, precision=highest, preferred_element_type=jnp.float32
        )
        owned_rows = lax.psum_scatter(dense_part, "wide", scatter_dimension=0, tiled=True)
        owner_block = lax.psum(owned_rows, "narrow").reshape(block_order, nrhs_count)
        solved = jnp.dot(
            inverse_block, owner_block, precision=highest, preferred_element_type=jnp.float32
        )
        all_solved = lax.all_gather(
            solved.reshape(capacity, basis_count * nrhs_count), "wide", axis=0, tiled=True
        )
        precond = finish(residual, all_solved)
        inner_value = lax.psum(jnp.sum(residual * precond, axis=(1, 2)), ("wide", "narrow"))
        return (precond, inner_value)

    residual = initial
    solution = jnp.zeros_like(initial)
    precond, inner_now = precondition(residual)
    direction = precond
    for iteration in range(ITERS):
        rounded = direction.astype(jnp.bfloat16)
        from_west = shifted(rounded[:, 0], "wide", 1)
        from_south = shifted(rounded[:, 1], "narrow", 1)
        west_face = jnp.dot(from_west, match_narrow[0], preferred_element_type=jnp.float32)
        south_face = jnp.dot(from_south, match_narrow[1], preferred_element_type=jnp.float32)
        stacked = jnp.stack(
            [
                rounded[:, 0].astype(jnp.float32),
                rounded[:, 1].astype(jnp.float32),
                west_face,
                south_face,
            ],
            axis=1,
        )
        slotted = jnp.einsum("rdk,ds->rsk", stacked, slot_table, precision=highest).astype(
            jnp.bfloat16
        )
        product = jnp.dot(
            slotted.reshape(nrhs_count, 4 * face_width), matrix, preferred_element_type=jnp.float32
        )
        by_face = jnp.einsum(
            "rsk,ds->rdk", product.reshape(nrhs_count, 4, face_width), slot_table, precision=highest
        )
        to_west = jnp.einsum("rk,mk->rm", by_face[:, 2], match_table[0], precision=highest)
        to_south = jnp.einsum("rk,mk->rm", by_face[:, 3], match_table[1], precision=highest)
        from_east = shifted(to_west, "wide", -1)
        from_north = shifted(to_south, "narrow", -1)
        summed_all = jnp.stack([by_face[:, 0] + from_east, by_face[:, 1] + from_north], axis=1)
        applied = summed_all * live_mask[None]
        curvature = lax.psum(jnp.sum(direction * applied, axis=(1, 2)), ("wide", "narrow"))
        step_size = inner_now / curvature
        solution = solution + step_size[:, None, None] * direction
        residual = residual - step_size[:, None, None] * applied
        if iteration + 1 < ITERS:
            precond, inner_new = precondition(residual)
            direction = precond + (inner_new / inner_now)[:, None, None] * direction
            inner_now = inner_new
    return (solution[None, None], residual[None, None])


def solution(mesh):
    placed = (
        P("wide", "narrow", None, None, None),
        P("wide", "narrow", None, None),
        P("wide", "narrow", None, None),
        P("wide", "narrow", None, None, None, None),
        P("wide", None, None),
        P("wide", "narrow", None),
        P("wide", "narrow", None, None),
        P("wide", "narrow", None),
        P(),
    )
    return jax.shard_map(
        body,
        mesh=mesh,
        in_specs=placed,
        out_specs=(P("wide", "narrow", None, None, None), P("wide", "narrow", None, None, None)),
        check_vma=False,
    )
```

profile of v0, /device:TPU:1, one launch (start us, length us, event | category | flops | bytes accessed | tf_op | source)
XLA Modules:
  0.0 640.1 jit_solution(5082868968421109135)
XLA Ops:
  10.6 2.1 pad_add_fusion
  16.4 110.0 %all-reduce.6.cloned.1.call-done = f32[320,128]{1,0:T(8,128)} async-done(((f32[320,128]{1,0:T(8,128)}), f32[320,128]{1,0:T(8,128)}) %all-reduce.6.cloned.1.call-update) | async-done | bytes 163856
  127.2 23.5 %psum.42 = f32[80,16]{1,0:T(8,128)S(1)} all-reduce(f32[80,16]{1,0:T(8,128)S(1)} %reshape.170), channel_id=1, replica_groups=mesh['wide'=32,'narrow'=8] {'narrow'}, use_global_device_ids=true, to_apply=%region_1.0 | all-reduce | flops 1280 | bytes 10240 | tf_op jit(solution)/shard_map/psum | solution.py:73
  151.1 30.1 %all-gather = f32[32,10,128]{2,1,0:T(8,128)S(1)} all-gather(f32[1,10,128]{2,1,0:T(8,128)S(1)} %reshape.179), channel_id=1, replica_groups=mesh['wide'=32,'narrow'=8] {'wide'}, dimensions={0}, use_global_device_ids=true | all-gather | bytes 168960 | tf_op jit(solution)/shard_map/all_gather | solution.py:77
  182.7 1.3 collective-permute-start.1
  185.3 12.3 %copy.57 = bf16[2048,2048]{1,0:T(8,128)(2,1)} copy(bf16[2048,2048]{0,1:T(8,128)(2,1)} %bitcast.206) | data formatting | bytes 16777216 | tf_op jit(solution)/shard_map/dot_general | solution.py:106
  197.6 2.6 collective-permute-start
  201.7 5.6 fusion.60
  208.9 1.3 collective-permute-start.3
  210.2 1.9 collective-permute-start.2
  212.1 2.1 collective-permute-done.3
  214.2 1.7 collective-permute-done.2
  216.1 78.5 %all-reduce.2 = (f32[16]{0:T(128)S(1)}, f32[16]{0:T(128)S(1)}) all-reduce(f32[16]{0:T(128)S(1)} %get-tuple-element.9, f32[16]{0:T(128)S(1)} %get-tuple-element.8), channel_id=1, replica_groups=mesh['wide'=32,'narrow'=8] {'wide','narrow'}, use_global_device_ids=true, to_apply=%region_3.0 | all-reduce | flops 32 | bytes 256 | tf_op jit(solution)/shard_map/psum | solution.py:81
  296.1 106.8 %all-reduce.8.cloned.1.call-done = f32[320,128]{1,0:T(8,128)} async-done(((f32[320,128]{1,0:T(8,128)}), f32[320,128]{1,0:T(8,128)}) %all-reduce.8.cloned.1.call-update) | async-done | bytes 163856
  403.7 23.5 %psum.45 = f32[80,16]{1,0:T(8,128)S(1)} all-reduce(f32[80,16]{1,0:T(8,128)S(1)} %reshape.175), channel_id=1, replica_groups=mesh['wide'=32,'narrow'=8] {'narrow'}, use_global_device_ids=true, to_apply=%region_7.0 | all-reduce | flops 1280 | bytes 10240 | tf_op jit(solution)/shard_map/psum | solution.py:73
  427.6 30.1 %all-gather.1 = f32[32,10,128]{2,1,0:T(8,128)S(1)} all-gather(f32[1,10,128]{2,1,0:T(8,128)S(1)} %reshape.181), channel_id=1, replica_groups=mesh['wide'=32,'narrow'=8] {'wide'}, dimensions={0}, use_global_device_ids=true | all-gather | bytes 168960 | tf_op jit(solution)/shard_map/all_gather | solution.py:77
  458.5 73.3 %psum.46 = f32[16]{0:T(128)S(1)} all-reduce(f32[16]{0:T(128)S(1)} %get-tuple-element.39), channel_id=1, replica_groups=mesh['wide'=32,'narrow'=8] {'wide','narrow'}, use_global_device_ids=true, to_apply=%region_9.0 | all-reduce | flops 16 | bytes 128 | tf_op jit(solution)/shard_map/psum | solution.py:81
  531.9 2.4 collective-permute-start.4
  534.4 3.9 collective-permute-start.5
  539.5 5.6 fusion.61
  546.7 1.3 collective-permute-start.7
  548.0 2.7 collective-permute-start.6
  551.6 1.6 collective-permute-done.6
  553.5 78.3 %psum.47 = f32[16]{0:T(128)S(1)} all-reduce(f32[16]{0:T(128)S(1)} %fusion.15), channel_id=1, replica_groups=mesh['wide'=32,'narrow'=8] {'wide','narrow'}, use_global_device_ids=true, to_apply=%region_11.0 | all-reduce | flops 16 | bytes 128 | tf_op jit(solution)/shard_map/psum | solution.py:118
  (79 shorter events, 22.3 us)
Async XLA Ops:
  7.2 143.6 %copy-start = (f32[1,80,80]{2,1,0:T(8,128)S(1)}, f32[1,80,80]{2,1,0:T(8,128)}, u32[]{:S(2)}) copy-start(f32[1,80,80]{2,1,0:T(8,128)} %param.13) | copy-start | bytes 76804
  7.2 119.2 %all-reduce.6.cloned.1.call-start = ((), (), s32[]{:S(2)}) async-start(), calls=%async_computation | async-start | bytes 327680
  13.7 389.2 %all-reduce.8.cloned.1.call-start = ((), (), s32[]{:S(2)}) async-start(), calls=%async_computation.1 | async-start | bytes 327680
  182.7 17.5 %collective-permute-start.1 = (bf16[16,512]{1,0:T(8,128)(2,1)S(1)}, bf16[16,512]{1,0:T(8,128)(2,1)S(1)}, u32[]{:S(2)}, u32[]{:S(2)}) collective-permute-start(bf16[16,512]{1,0:T(8,128)(2,1)S(1)} %get-tuple-element.30), channel_id=1, source_target_pairs={{0,1},{1,2},{2,3},{3,4},{4,5},{5,6},{6,7},{8,9},{9,10},{10,11},{11... | collective-permute-start | bytes 49160 | tf_op jit(solution)/shard_map/ppermute | solution.py:13
  185.3 16.0 %copy-start.3 = (s32[1,1,4]{2,1,0:T(1,128)S(1)}, s32[1,1,4]{2,1,0:T(1,128)}, u32[]{:S(2)}) copy-start(s32[1,1,4]{2,1,0:T(1,128)} %param.16) | copy-start | bytes 52
  197.6 18.4 %copy-start.1 = (f32[1,1,16,2,512]{4,3,2,1,0:T(2,128)S(1)}, f32[1,1,16,2,512]{4,3,2,1,0:T(2,128)}, u32[]{:S(2)}) copy-start(f32[1,1,16,2,512]{4,3,2,1,0:T(2,128)} %param.9) | copy-start | bytes 196612
  197.6 97.1 %copy-start.2 = (f32[1,1,2,2,8,512]{5,4,3,2,1,0:T(8,128)S(1)}, f32[1,1,2,2,8,512]{5,4,3,2,1,0:T(8,128)}, u32[]{:S(2)}) copy-start(f32[1,1,2,2,8,512]{5,4,3,2,1,0:T(8,128)} %param.12) | copy-start | bytes 196612
  197.6 3.4 collective-permute-start
  208.9 5.4 collective-permute-start.3
  210.2 5.8 collective-permute-start.2
  531.9 6.3 collective-permute-start.4
  534.4 4.5 collective-permute-start.5
  546.7 4.9 collective-permute-start.7
  548.0 5.2 collective-permute-start.6
Sparse Core Ops, SparseCore 0:
  13.8 112.5 all-reduce.5
  296.3 106.6 all-reduce.7
where the time goes:
time: 641 us; the launch traced here: 640 us
  blocking collectives  337 us (53%)
  waiting for transfers between devices  224 us (35%)
  matrix products  21.5 us (3%)
  local copies, waits for them, and re-layouts  18.9 us (3%)
  starting transfers between devices  17.5 us (3%)
  between operations  15 us (2%)
    unnamed x4, waiting for transfers between devices  217 us
    psum x2, blocking collectives, precondition(): lax.psum(jnp.sum(residual * precond, axis=(1, 2)), ('wide', 'narrow'))  152 us
    psum x1, blocking collectives, body(): lax.psum(jnp.sum(direction * applied, axis=(1, 2)), ('wide', 'narrow'))  78.3 us
    all_gather x2, blocking collectives, precondition(): lax.all_gather(solved.reshape(capacity, basis_count * nrhs_count), 'wide'...  60.2 us
    psum x2, blocking collectives, precondition(): lax.psum(owned_rows, 'narrow').reshape(block_order, nrhs_count)  47.1 us
    ppermute x8, starting transfers between devices, shifted(): return lax.ppermute(block, axis, route)  17.5 us
  transfers between devices with their start and end apart: 10, of which 8 were waited for; matrix products, arithmetic and copies ran while one was open for 2% of the time, Pallas kernels for 0%

commit v1 on v0

--- a/solution.py
+++ b/solution.py
@@ -78,7 +78,7 @@
             solved.reshape(capacity, basis_count * nrhs_count), "wide", axis=0, tiled=True
         )
         precond = finish(residual, all_solved)
-        inner_value = lax.psum(jnp.sum(residual * precond, axis=(1, 2)), ("wide", "narrow"))
+        inner_value = lax.psum(lax.psum(jnp.sum(residual * precond, axis=(1, 2)), "wide"), "narrow")
         return (precond, inner_value)
 
     residual = initial

time: 641 us -> 721 us (1.12)
  blocking collectives: 337 us -> 412 us
    psum x1 -> x2, blocking collectives: 78.3 us -> 155 us  [body(): lax.psum(jnp.sum(direction * applied, axis=(1, 2)), ('wide', 'narrow'))]
    psum x2 -> x4, blocking collectives: 152 us -> 150 us  [the longest x2 125 us: precondition(): lax.psum(jnp.sum(residual * precond, axis=(1, 2)), 'wide')]
  transfers between devices with their start and end apart: 10 -> 10, of which waited for: 8 -> 7; matrix products, arithmetic and copies ran while one was open for 2% -> 2% of each run, Pallas kernels for 0% -> 0%
where the time goes in v1:
time: 721 us; the launch traced here: 719 us
  blocking collectives  412 us (57%)
  waiting for transfers between devices  225 us (31%)
  starting transfers between devices  21.7 us (3%)
  matrix products  21.6 us (3%)
  local copies, waits for them, and re-layouts  18.9 us (3%)
  between operations  15 us (2%)
    unnamed x4, waiting for transfers between devices  218 us
    psum x2, blocking collectives, body(): lax.psum(jnp.sum(direction * applied, axis=(1, 2)), ('wide', 'narrow'))  155 us
    psum x2, blocking collectives, precondition(): lax.psum(jnp.sum(residual * precond, axis=(1, 2)), 'wide')  125 us
    all_gather x2, blocking collectives, precondition(): lax.all_gather(solved.reshape(capacity, basis_count * nrhs_count), 'wide'...  60.2 us
    psum x2, blocking collectives, precondition(): lax.psum(owned_rows, 'narrow').reshape(block_order, nrhs_count)  47.1 us
    psum x2, blocking collectives, precondition(): lax.psum(lax.psum(jnp.sum(residual * precond, axis=(1, 2)), 'wide'), 'nar...  24.9 us
    ppermute x8, starting transfers between devices, shifted(): return lax.ppermute(block, axis, route)  21.6 us
  transfers between devices with their start and end apart: 10, of which 7 were waited for; matrix products, arithmetic and copies ran while one was open for 2% of the time, Pallas kernels for 0%

profile of v1, /device:TPU:1, one launch (start us, length us, event | category | flops | bytes accessed | tf_op | source)
XLA Modules:
  0.0 719.4 jit_solution(11488864051746506509)
XLA Ops:
  10.6 2.1 pad_add_fusion
  16.4 110.0 %all-reduce.5.cloned.1.call-done = f32[320,128]{1,0:T(8,128)} async-done(((f32[320,128]{1,0:T(8,128)}), f32[320,128]{1,0:T(8,128)}) %all-reduce.5.cloned.1.call-update) | async-done | bytes 163856
  127.2 23.5 %psum.56 = f32[80,16]{1,0:T(8,128)S(1)} all-reduce(f32[80,16]{1,0:T(8,128)S(1)} %reshape.170), channel_id=1, replica_groups=mesh['wide'=32,'narrow'=8] {'narrow'}, use_global_device_ids=true, to_apply=%region_1.0 | all-reduce | flops 1280 | bytes 10240 | tf_op jit(solution)/shard_map/psum | solution.py:73
  151.1 30.1 %all-gather = f32[32,10,128]{2,1,0:T(8,128)S(1)} all-gather(f32[1,10,128]{2,1,0:T(8,128)S(1)} %reshape.179), channel_id=1, replica_groups=mesh['wide'=32,'narrow'=8] {'wide'}, dimensions={0}, use_global_device_ids=true | all-gather | bytes 168960 | tf_op jit(solution)/shard_map/all_gather | solution.py:77
  182.7 1.3 collective-permute-start.1
  185.3 12.3 %copy.57 = bf16[2048,2048]{1,0:T(8,128)(2,1)} copy(bf16[2048,2048]{0,1:T(8,128)(2,1)} %bitcast.206) | data formatting | bytes 16777216 | tf_op jit(solution)/shard_map/dot_general | solution.py:106
  197.6 2.6 collective-permute-start
  201.7 5.6 fusion.60
  210.2 1.9 collective-permute-start.2
  212.1 2.1 collective-permute-done.3
  214.2 1.7 collective-permute-done.2
  216.1 78.6 %psum.59 = f32[16]{0:T(128)S(1)} all-reduce(f32[16]{0:T(128)S(1)} %get-tuple-element.8), channel_id=1, replica_groups=mesh['wide'=32,'narrow'=8] {'wide','narrow'}, use_global_device_ids=true, to_apply=%region_6.0 | all-reduce | flops 16 | bytes 128 | tf_op jit(solution)/shard_map/psum | solution.py:118
  294.7 62.7 %psum.57 = f32[16]{0:T(128)S(1)} all-reduce(f32[16]{0:T(128)S(1)} %get-tuple-element.9), channel_id=1, replica_groups=mesh['wide'=32,'narrow'=8] {'wide'}, use_global_device_ids=true, to_apply=%region_3.0 | all-reduce | flops 16 | bytes 128 | tf_op jit(solution)/shard_map/psum | solution.py:81
  357.4 13.4 %psum.58 = f32[16]{0:T(128)S(1)} all-reduce(f32[16]{0:T(128)S(1)} %psum.57), channel_id=1, replica_groups=mesh['wide'=32,'narrow'=8] {'narrow'}, use_global_device_ids=true, to_apply=%region_4.0 | all-reduce | flops 16 | bytes 128 | tf_op jit(solution)/shard_map/psum | solution.py:81
  372.3 108.1 %all-reduce.7.cloned.1.call-done = f32[320,128]{1,0:T(8,128)} async-done(((f32[320,128]{1,0:T(8,128)}), f32[320,128]{1,0:T(8,128)}) %all-reduce.7.cloned.1.call-update) | async-done | bytes 163856
  481.2 23.5 %psum.60 = f32[80,16]{1,0:T(8,128)S(1)} all-reduce(f32[80,16]{1,0:T(8,128)S(1)} %reshape.175), channel_id=1, replica_groups=mesh['wide'=32,'narrow'=8] {'narrow'}, use_global_device_ids=true, to_apply=%region_8.0 | all-reduce | flops 1280 | bytes 10240 | tf_op jit(solution)/shard_map/psum | solution.py:73
  505.1 30.1 %all-gather.1 = f32[32,10,128]{2,1,0:T(8,128)S(1)} all-gather(f32[1,10,128]{2,1,0:T(8,128)S(1)} %reshape.181), channel_id=1, replica_groups=mesh['wide'=32,'narrow'=8] {'wide'}, dimensions={0}, use_global_device_ids=true | all-gather | bytes 168960 | tf_op jit(solution)/shard_map/all_gather | solution.py:77
  536.0 62.2 %psum.61 = f32[16]{0:T(128)S(1)} all-reduce(f32[16]{0:T(128)S(1)} %get-tuple-element.37), channel_id=1, replica_groups=mesh['wide'=32,'narrow'=8] {'wide'}, use_global_device_ids=true, to_apply=%region_10.0 | all-reduce | flops 16 | bytes 128 | tf_op jit(solution)/shard_map/psum | solution.py:81
  598.2 11.5 %psum.62 = f32[16]{0:T(128)S(1)} all-reduce(f32[16]{0:T(128)S(1)} %psum.61), channel_id=1, replica_groups=mesh['wide'=32,'narrow'=8] {'narrow'}, use_global_device_ids=true, to_apply=%region_11.0 | all-reduce | flops 16 | bytes 128 | tf_op jit(solution)/shard_map/psum | solution.py:81
  609.8 4.8 collective-permute-start.4
  614.5 2.9 collective-permute-start.5
  619.4 5.6 fusion.61
  627.8 5.5 collective-permute-start.6
  634.4 76.6 %psum.63 = f32[16]{0:T(128)S(1)} all-reduce(f32[16]{0:T(128)S(1)} %fusion.15), channel_id=1, replica_groups=mesh['wide'=32,'narrow'=8] {'wide','narrow'}, use_global_device_ids=true, to_apply=%region_13.0 | all-reduce | flops 16 | bytes 128 | tf_op jit(solution)/shard_map/psum | solution.py:118
  (82 shorter events, 25.5 us)
Async XLA Ops:
  7.2 143.6 %copy-start = (f32[1,80,80]{2,1,0:T(8,128)S(1)}, f32[1,80,80]{2,1,0:T(8,128)}, u32[]{:S(2)}) copy-start(f32[1,80,80]{2,1,0:T(8,128)} %param.13) | copy-start | bytes 76804
  7.2 119.2 %all-reduce.5.cloned.1.call-start = ((), (), s32[]{:S(2)}) async-start(), calls=%async_computation | async-start | bytes 327680
  13.7 466.7 %all-reduce.7.cloned.1.call-start = ((), (), s32[]{:S(2)}) async-start(), calls=%async_computation.1 | async-start | bytes 327680
  182.7 17.5 %collective-permute-start.1 = (bf16[16,512]{1,0:T(8,128)(2,1)S(1)}, bf16[16,512]{1,0:T(8,128)(2,1)S(1)}, u32[]{:S(2)}, u32[]{:S(2)}) collective-permute-start(bf16[16,512]{1,0:T(8,128)(2,1)S(1)} %get-tuple-element.28), channel_id=1, source_target_pairs={{0,1},{1,2},{2,3},{3,4},{4,5},{5,6},{6,7},{8,9},{9,10},{10,11},{11... | collective-permute-start | bytes 49160 | tf_op jit(solution)/shard_map/ppermute | solution.py:13
  185.3 16.0 %copy-start.3 = (s32[1,1,4]{2,1,0:T(1,128)S(1)}, s32[1,1,4]{2,1,0:T(1,128)}, u32[]{:S(2)}) copy-start(s32[1,1,4]{2,1,0:T(1,128)} %param.16) | copy-start | bytes 52
  197.6 18.4 %copy-start.1 = (f32[1,1,16,2,512]{4,3,2,1,0:T(2,128)S(1)}, f32[1,1,16,2,512]{4,3,2,1,0:T(2,128)}, u32[]{:S(2)}) copy-start(f32[1,1,16,2,512]{4,3,2,1,0:T(2,128)} %param.9) | copy-start | bytes 196612
  197.6 173.2 %copy-start.2 = (f32[1,1,2,2,8,512]{5,4,3,2,1,0:T(8,128)S(1)}, f32[1,1,2,2,8,512]{5,4,3,2,1,0:T(8,128)}, u32[]{:S(2)}) copy-start(f32[1,1,2,2,8,512]{5,4,3,2,1,0:T(8,128)} %param.12) | copy-start | bytes 196612
  197.6 3.4 collective-permute-start
  208.9 5.4 collective-permute-start.3
  210.2 5.8 collective-permute-start.2
  609.8 8.7 %collective-permute-start.4 = (bf16[16,512]{1,0:T(8,128)(2,1)S(1)}, bf16[16,512]{1,0:T(8,128)(2,1)S(1)}, u32[]{:S(2)}, u32[]{:S(2)}) collective-permute-start(bf16[16,512]{1,0:T(8,128)(2,1)S(1)} %get-tuple-element.23), channel_id=1, source_target_pairs={{0,8},{8,16},{16,24},{24,32},{32,40},{40,48},{48,56},{56,64},{64,7... | collective-permute-start | bytes 49160 | tf_op jit(solution)/shard_map/ppermute | solution.py:13
  614.5 4.2 collective-permute-start.5
  626.5 6.8 collective-permute-start.7
  627.8 6.4 collective-permute-start.6
Sparse Core Ops, SparseCore 0:
  13.8 112.5 all-reduce.4
  372.4 107.9 all-reduce.6
